TPU v7x, 32 devices: a whole 2x2x4 slice. The times are simulated.
32 devices in a mesh: batch: 4 (over z), seq: 8 (over y, x, core).
Axes of the slice: x: 2, y: 2, z: 4, core: 2. Of those that a mesh axis runs over, the one named last changes fastest.
Arguments:
- queries: bfloat16 [16384, 8, 256], P(('batch', 'seq')), parts along dimension 0, may hold values from -400 to 400
- key_heads: bfloat16 [16384, 4, 256], P(('batch', 'seq')), parts along dimension 0, may hold values from -16 to 16
- projected_value_heads: bfloat16 [16384, 4, 256], P(('batch', 'seq')), parts along dimension 0, may hold values from -6 to 6
- lengths: int32 [4], P('batch'), parts along dimension 0, may hold values from 3585 to 4096
Outputs:
- attended: bfloat16 [16384, 8, 256], P(('batch', 'seq')), parts along dimension 0
There are 4 independent parts, one for each index of `batch`. A program takes and returns all parts, laid end to end along the dimension named above; each array names one. Nothing has to cross between parts.
All inputs are finite; a program needn't handle non-finite values.
Results may differ from a plain program's by a relative error of at most 0.0033.
Values may be sent and summed in bfloat16 or wider, within the bound.
No kernel may reach another device: no remote copies, remote signals or barrier semaphores. Data moves between devices by JAX's collectives and lax.ppermute only.
A program may use at most 192 MiB of HBM per device.

v0:
```python
import math
import jax
import jax.numpy as jnp
from jax import lax
from jax.sharding import PartitionSpec as P

WINDOW = 4096
SINKS = 4


def spread(value, axis, source):
    kept = jnp.where(lax.axis_index(axis) == source, value, 0).astype(value.dtype)
    return lax.psum(kept, axis)


def shards(queries, key_heads, projected_value_heads, lengths):
    tok_rows = queries.shape[0]
    head_count = queries.shape[1]
    head_width = queries.shape[2]
    kv_heads = key_heads.shape[1]
    share = head_count // kv_heads
    position = lax.axis_index("seq")
    length_now = lengths[0]
    first_row = position * tok_rows
    score_scale = head_width ** (-0.5)
    grouped = queries.reshape(tok_rows, kv_heads, share, head_width)
    query_pos = first_row + jnp.arange(tok_rows, dtype=jnp.int32)
    last_query = first_row + tok_rows - 1

    def attend(running, kv_block, key_start, sink_mode):
        key_count = kv_block.shape[1]
        key_pos = key_start + jnp.arange(key_count, dtype=jnp.int32)
        if sink_mode:
            useful = first_row < length_now
        else:
            useful = (
                (key_start <= last_query)
                & (key_start + key_count - 1 > first_row - WINDOW)
                & (key_start < length_now)
                & (first_row < length_now)
                & (key_start + key_count > SINKS)
            )

        def compute(current):
            maximum, totals, weighted = current
            scores = (
                jnp.einsum(
                    "qhgd,khd->hgqk", grouped, kv_block[0], preferred_element_type=jnp.float32
                )
                * score_scale
            )
            distance = query_pos[:, None] - key_pos[None, :]
            if sink_mode:
                visible = (distance >= 0) & (key_pos[None, :] < length_now)
            else:
                visible = (
                    (distance >= 0)
                    & (distance < WINDOW)
                    & (key_pos[None, :] >= SINKS)
                    & (key_pos[None, :] < length_now)
                )
            visible = visible & (query_pos[:, None] < length_now)
            masked = jnp.where(visible, scores, -1e30)
            newest = jnp.maximum(maximum, jnp.max(masked, axis=-1))
            weights = jnp.where(visible, jnp.exp(scores - newest[..., None]), 0.0)
            rescale = jnp.exp(maximum - newest)
            totals = totals * rescale + jnp.sum(weights, axis=-1)
            weighted = weighted * rescale[..., None] + jnp.einsum(
                "hgqk,khd->hgqd",
                weights.astype(jnp.bfloat16),
                kv_block[1],
                preferred_element_type=jnp.float32,
            )
            return (newest, totals, weighted)

        return lax.cond(useful, compute, lambda current: current, running)

    running = (
        jnp.full((kv_heads, share, tok_rows), -1e30, jnp.float32),
        jnp.zeros((kv_heads, share, tok_rows), jnp.float32),
        jnp.zeros((kv_heads, share, tok_rows, head_width), jnp.float32),
    )
    own_pair = jnp.stack([key_heads, projected_value_heads])
    sink_pair = spread(own_pair[:, :SINKS], "seq", 0)
    running = attend(running, sink_pair, jnp.int32(0), True)
    shard_piece = lax.all_gather(own_pair, "seq", axis=1, tiled=True)
    piece_rows = shard_piece.shape[1]
    block_size = math.gcd(piece_rows, tok_rows)

    def one_slice(slice_index, inner):
        sliced = lax.dynamic_slice_in_dim(shard_piece, slice_index * block_size, block_size, 1)
        return attend(inner, sliced, slice_index * block_size, False)

    running = lax.fori_loop(0, piece_rows // block_size, one_slice, running)
    maximum, totals, weighted = running
    valid = query_pos < length_now
    result = jnp.where(valid[:, None], weighted / jnp.where(valid, totals, 1.0)[..., None], 0.0)
    return (
        result.transpose(2, 0, 1, 3).reshape(tok_rows, head_count, head_width).astype(jnp.bfloat16)
    )


def solution(mesh):
    in_specs = (
        P(("batch", "seq"), None, None),
        P(("batch", "seq"), None, None),
        P(("batch", "seq"), None, None),
        P("batch"),
    )
    out_specs = P(("batch", "seq"), None, None)
    return jax.shard_map(shards, mesh=mesh, in_specs=in_specs, out_specs=out_specs, check_vma=False)
```

profile of v0, /device:TPU:7, one launch (start us, length us, event | category | flops | bytes accessed | tf_op | source)
XLA Modules:
  0.0 233.9 jit_solution(17987228410753566416)
XLA Ops:
  6.5 1.8 copy_bitcast_fusion
  8.4 1.5 pad_maximum_fusion
  10.5 3.3 %copy.8 = bf16[512,8,256]{2,0,1:T(8,128)(2,1)} copy(bf16[512,8,256]{2,1,0:T(8,128)(2,1)} %param.10) | data formatting | bytes 4194304 | tf_op args[0]
  13.9 23.0 %psum.7 = bf16[2,4,4,256]{3,1,2,0:T(4,128)(2,1)S(1)} all-reduce(bf16[2,4,4,256]{3,1,2,0:T(4,128)(2,1)S(1)} %fusion.40), channel_id=1, replica_groups=mesh['batch'=4,'seq'=8] {'seq'}, use_global_device_ids=true, to_apply=%region_0.1 | all-reduce | flops 8192 | bytes 32768 | tf_op jit(solution)/shard_map/psum | solution.py:13
  36.9 9.0 %conditional.2 = (f32[4,2,512]{2,1,0:T(2,128)}, f32[4,2,512]{2,1,0:T(2,128)S(1)}, f32[4,2,512,256]{3,2,1,0:T(8,128)}) conditional(s32[]{:T(128)} %convert_element_type.35, () %tuple.61, (s32[512]{0:T(512)S(1)}, s32[4]{0:T(128)S(1)}, s32[]{:T(128)}, s32[4]{0:T(128)S(1)}, bf16[2,4,4,256]{3,1,2,0:T(4,128)(2,1)S(1)}, ...), branch_computations={%region_1.2_spmd, %region_2.5_spmd} | conditional | flops 17998340 | bytes 6698056 | solution.py:76
  38.3 2.3 select_reduce_fusion
  41.2 0.8 fusion.4
  42.0 0.7 fusion.16
  42.8 3.2 %convolution_add_fusion = f32[4,2,512,256]{3,2,1,0:T(8,128)} fusion(f32[4,2,512]{2,1,0:T(2,128)S(1)} %get-tuple-element.538, f32[4,2,512,4]{2,3,1,0:T(4,128)S(1)} %get-tuple-element.547, f32[4,2,512]{2,1,0:T(2,128)} %get-tuple-element.637, pred[512,4]{0,1:T(4,128)(4,1)S(1)} %fusion.14, bf16[2,4,4,256]{3,1,2,0:T(4,128)(2,1)S(1)} %get-tuple-element.449), kind=kOutput, calls=%fused_computation.1 | convolution fusion | flops 9486336 | bytes 4302848 | tf_op jit(solution)/shard_map/cond/branch_1_fun/hgqk,khd->hgqd/dot_general | solution.py:68
  46.0 54.7 %all-gather.2.cloned.1.call-done = bf16[2,4096,4,256]{3,1,2,0:T(8,128)(2,1)} async-done(((bf16[2,512,4,256]{3,1,2,0:T(8,128)(2,1)}), bf16[2,4096,4,256]{3,1,2,0:T(8,128)(2,1)}) %all-gather.2.cloned.1.call-update) | async-done | bytes 16777232 | tf_op jit(solution)/shard_map/all_gather | solution.py:86
  100.6 121.3 %while.22 = (s32[]{:T(128)}, f32[4,2,512]{2,1,0:T(2,128)}, f32[4,2,512]{2,1,0:T(2,128)S(1)}, f32[4,2,512,256]{3,2,1,0:T(8,128)}, s32[]{:T(128)}, /*index=5*/s32[...) while((s32[]{:T(128)}, f32[4,2,512]{2,1,0:T(2,128)}, ...), condition=%wide.region_10.11_spmd.clone, body=%wide.region_5.10_spmd.clone.sunk | while | flops 2174495232 | bytes 39079348 | solution.py:94
  101.3 14.5 %conditional.5 = ((f32[4,2,512]{2,1,0:T(2,128)}, f32[4,2,512]{2,1,0:T(2,128)S(1)}, f32[4,2,512,256]{3,2,1,0:T(8,128)})) conditional(s32[]{:T(128)} %convert_element_type.48, (f32[4,2,512]{2,1,0:T(2,128)}, f32[4,2,512]{2,1,0:T(2,128)S(1)}, f32[4,2,512,256]{3,2,1,0:T(8,128)}) %tuple.88, (s32[]{:T(128)}, s32[]{:T(128)}, s32[512]{0:T(512)S(1)}, ...), branch_computations={%region_6.6_spmd, %region_7.9_spmd} | conditional | flops 2174495232 | bytes 39076968 | solution.py:76
  101.3 0.7 broadcast_compare_fusion.2
  102.4 3.5 %fusion.17 = (f32[4,2,512]{2,1,0:T(2,128)S(1)}, f32[4,512,512,2]{2,1,3,0:T(8,128)S(1)}) fusion(pred[512,512]{0,1:T(8,128)(4,1)S(1)} %fusion.34, bf16[512,4,2,256]{3,0,2,1:T(8,128)(2,1)} %get-tuple-element.457, bf16[2,4096,4,256]{3,1,2,0:T(8,128)(2,1)} %get-tuple-element.456, s32[]{:T(128)S(6)} %select_n.38), kind=kOutput, calls=%fused_computation.26 | convolution fusion | flops 1080029184 | bytes 11812868 | tf_op jit(solution)/shard_map/while/body/eval_jaxpr/cond/branch_1_fun/qhgd,khd->hgqk/dot_general | solution.py:47
  105.9 0.7 max.4
  106.6 1.7 fusion.21
  108.3 0.7 multiply_add_fusion.1
  109.1 6.1 %multiply_add_fusion = f32[4,2,512,256]{3,2,1,0:T(8,128)} fusion(f32[4,2,512,256]{3,2,1,0:T(8,128)} %get-tuple-element.459, f32[4,2,512]{2,1,0:T(2,128)S(1)} %bitcast.69, f32[4,512,512,2]{2,1,3,0:T(8,128)S(1)} %get-tuple-element.549, f32[4,2,512]{2,1,0:T(2,128)S(1)} %max.4, pred[512,512]{0,1:T(8,128)(4,1)S(1)} %fusion.34, ...), kind=kOutput, calls=%fused_computation.32 | convolution fusion | flops 1084227584 | bytes 18120712 | tf_op jit(solution)/shard_map/while/body/eval_jaxpr/cond/branch_1_fun/hgqk,khd->hgqd/dot_general | solution.py:68
  116.4 14.5 %conditional.5 = ((f32[4,2,512]{2,1,0:T(2,128)}, f32[4,2,512]{2,1,0:T(2,128)S(1)}, f32[4,2,512,256]{3,2,1,0:T(8,128)})) conditional(s32[]{:T(128)} %convert_element_type.48, (f32[4,2,512]{2,1,0:T(2,128)}, f32[4,2,512]{2,1,0:T(2,128)S(1)}, f32[4,2,512,256]{3,2,1,0:T(8,128)}) %tuple.88, (s32[]{:T(128)}, s32[]{:T(128)}, s32[512]{0:T(512)S(1)}, ...), branch_computations={%region_6.6_spmd, %region_7.9_spmd} | conditional | flops 2174495232 | bytes 39076968 | solution.py:76
  116.5 0.7 broadcast_compare_fusion.2
  117.6 3.5 %fusion.17 = (f32[4,2,512]{2,1,0:T(2,128)S(1)}, f32[4,512,512,2]{2,1,3,0:T(8,128)S(1)}) fusion(pred[512,512]{0,1:T(8,128)(4,1)S(1)} %fusion.34, bf16[512,4,2,256]{3,0,2,1:T(8,128)(2,1)} %get-tuple-element.457, bf16[2,4096,4,256]{3,1,2,0:T(8,128)(2,1)} %get-tuple-element.456, s32[]{:T(128)S(6)} %select_n.38), kind=kOutput, calls=%fused_computation.26 | convolution fusion | flops 1080029184 | bytes 11812868 | tf_op jit(solution)/shard_map/while/body/eval_jaxpr/cond/branch_1_fun/qhgd,khd->hgqk/dot_general | solution.py:47
  121.0 0.7 max.4
  121.8 1.7 fusion.21
  123.5 0.7 multiply_add_fusion.1
  124.2 6.1 %multiply_add_fusion = f32[4,2,512,256]{3,2,1,0:T(8,128)} fusion(f32[4,2,512,256]{3,2,1,0:T(8,128)} %get-tuple-element.459, f32[4,2,512]{2,1,0:T(2,128)S(1)} %bitcast.69, f32[4,512,512,2]{2,1,3,0:T(8,128)S(1)} %get-tuple-element.549, f32[4,2,512]{2,1,0:T(2,128)S(1)} %max.4, pred[512,512]{0,1:T(8,128)(4,1)S(1)} %fusion.34, ...), kind=kOutput, calls=%fused_computation.32 | convolution fusion | flops 1084227584 | bytes 18120712 | tf_op jit(solution)/shard_map/while/body/eval_jaxpr/cond/branch_1_fun/hgqk,khd->hgqd/dot_general | solution.py:68
  131.6 14.5 %conditional.5 = ((f32[4,2,512]{2,1,0:T(2,128)}, f32[4,2,512]{2,1,0:T(2,128)S(1)}, f32[4,2,512,256]{3,2,1,0:T(8,128)})) conditional(s32[]{:T(128)} %convert_element_type.48, (f32[4,2,512]{2,1,0:T(2,128)}, f32[4,2,512]{2,1,0:T(2,128)S(1)}, f32[4,2,512,256]{3,2,1,0:T(8,128)}) %tuple.88, (s32[]{:T(128)}, s32[]{:T(128)}, s32[512]{0:T(512)S(1)}, ...), branch_computations={%region_6.6_spmd, %region_7.9_spmd} | conditional | flops 2174495232 | bytes 39076968 | solution.py:76
  131.6 0.7 broadcast_compare_fusion.2
  132.7 3.5 %fusion.17 = (f32[4,2,512]{2,1,0:T(2,128)S(1)}, f32[4,512,512,2]{2,1,3,0:T(8,128)S(1)}) fusion(pred[512,512]{0,1:T(8,128)(4,1)S(1)} %fusion.34, bf16[512,4,2,256]{3,0,2,1:T(8,128)(2,1)} %get-tuple-element.457, bf16[2,4096,4,256]{3,1,2,0:T(8,128)(2,1)} %get-tuple-element.456, s32[]{:T(128)S(6)} %select_n.38), kind=kOutput, calls=%fused_computation.26 | convolution fusion | flops 1080029184 | bytes 11812868 | tf_op jit(solution)/shard_map/while/body/eval_jaxpr/cond/branch_1_fun/qhgd,khd->hgqk/dot_general | solution.py:47
  136.2 0.7 max.4
  136.9 1.7 fusion.21
  138.7 0.7 multiply_add_fusion.1
  139.4 6.1 %multiply_add_fusion = f32[4,2,512,256]{3,2,1,0:T(8,128)} fusion(f32[4,2,512,256]{3,2,1,0:T(8,128)} %get-tuple-element.459, f32[4,2,512]{2,1,0:T(2,128)S(1)} %bitcast.69, f32[4,512,512,2]{2,1,3,0:T(8,128)S(1)} %get-tuple-element.549, f32[4,2,512]{2,1,0:T(2,128)S(1)} %max.4, pred[512,512]{0,1:T(8,128)(4,1)S(1)} %fusion.34, ...), kind=kOutput, calls=%fused_computation.32 | convolution fusion | flops 1084227584 | bytes 18120712 | tf_op jit(solution)/shard_map/while/body/eval_jaxpr/cond/branch_1_fun/hgqk,khd->hgqd/dot_general | solution.py:68
  146.8 14.5 %conditional.5 = ((f32[4,2,512]{2,1,0:T(2,128)}, f32[4,2,512]{2,1,0:T(2,128)S(1)}, f32[4,2,512,256]{3,2,1,0:T(8,128)})) conditional(s32[]{:T(128)} %convert_element_type.48, (f32[4,2,512]{2,1,0:T(2,128)}, f32[4,2,512]{2,1,0:T(2,128)S(1)}, f32[4,2,512,256]{3,2,1,0:T(8,128)}) %tuple.88, (s32[]{:T(128)}, s32[]{:T(128)}, s32[512]{0:T(512)S(1)}, ...), branch_computations={%region_6.6_spmd, %region_7.9_spmd} | conditional | flops 2174495232 | bytes 39076968 | solution.py:76
  147.9 3.5 %fusion.17 = (f32[4,2,512]{2,1,0:T(2,128)S(1)}, f32[4,512,512,2]{2,1,3,0:T(8,128)S(1)}) fusion(pred[512,512]{0,1:T(8,128)(4,1)S(1)} %fusion.34, bf16[512,4,2,256]{3,0,2,1:T(8,128)(2,1)} %get-tuple-element.457, bf16[2,4096,4,256]{3,1,2,0:T(8,128)(2,1)} %get-tuple-element.456, s32[]{:T(128)S(6)} %select_n.38), kind=kOutput, calls=%fused_computation.26 | convolution fusion | flops 1080029184 | bytes 11812868 | tf_op jit(solution)/shard_map/while/body/eval_jaxpr/cond/branch_1_fun/qhgd,khd->hgqk/dot_general | solution.py:47
  151.4 0.7 max.4
  152.1 1.7 fusion.21
  153.8 0.7 multiply_add_fusion.1
  154.6 6.1 %multiply_add_fusion = f32[4,2,512,256]{3,2,1,0:T(8,128)} fusion(f32[4,2,512,256]{3,2,1,0:T(8,128)} %get-tuple-element.459, f32[4,2,512]{2,1,0:T(2,128)S(1)} %bitcast.69, f32[4,512,512,2]{2,1,3,0:T(8,128)S(1)} %get-tuple-element.549, f32[4,2,512]{2,1,0:T(2,128)S(1)} %max.4, pred[512,512]{0,1:T(8,128)(4,1)S(1)} %fusion.34, ...), kind=kOutput, calls=%fused_computation.32 | convolution fusion | flops 1084227584 | bytes 18120712 | tf_op jit(solution)/shard_map/while/body/eval_jaxpr/cond/branch_1_fun/hgqk,khd->hgqd/dot_general | solution.py:68
  161.9 14.5 %conditional.5 = ((f32[4,2,512]{2,1,0:T(2,128)}, f32[4,2,512]{2,1,0:T(2,128)S(1)}, f32[4,2,512,256]{3,2,1,0:T(8,128)})) conditional(s32[]{:T(128)} %convert_element_type.48, (f32[4,2,512]{2,1,0:T(2,128)}, f32[4,2,512]{2,1,0:T(2,128)S(1)}, f32[4,2,512,256]{3,2,1,0:T(8,128)}) %tuple.88, (s32[]{:T(128)}, s32[]{:T(128)}, s32[512]{0:T(512)S(1)}, ...), branch_computations={%region_6.6_spmd, %region_7.9_spmd} | conditional | flops 2174495232 | bytes 39076968 | solution.py:76
  163.0 3.5 %fusion.17 = (f32[4,2,512]{2,1,0:T(2,128)S(1)}, f32[4,512,512,2]{2,1,3,0:T(8,128)S(1)}) fusion(pred[512,512]{0,1:T(8,128)(4,1)S(1)} %fusion.34, bf16[512,4,2,256]{3,0,2,1:T(8,128)(2,1)} %get-tuple-element.457, bf16[2,4096,4,256]{3,1,2,0:T(8,128)(2,1)} %get-tuple-element.456, s32[]{:T(128)S(6)} %select_n.38), kind=kOutput, calls=%fused_computation.26 | convolution fusion | flops 1080029184 | bytes 11812868 | tf_op jit(solution)/shard_map/while/body/eval_jaxpr/cond/branch_1_fun/qhgd,khd->hgqk/dot_general | solution.py:47
  166.5 0.7 max.4
  167.2 1.7 fusion.21
  169.0 0.7 multiply_add_fusion.1
  169.7 6.1 %multiply_add_fusion = f32[4,2,512,256]{3,2,1,0:T(8,128)} fusion(f32[4,2,512,256]{3,2,1,0:T(8,128)} %get-tuple-element.459, f32[4,2,512]{2,1,0:T(2,128)S(1)} %bitcast.69, f32[4,512,512,2]{2,1,3,0:T(8,128)S(1)} %get-tuple-element.549, f32[4,2,512]{2,1,0:T(2,128)S(1)} %max.4, pred[512,512]{0,1:T(8,128)(4,1)S(1)} %fusion.34, ...), kind=kOutput, calls=%fused_computation.32 | convolution fusion | flops 1084227584 | bytes 18120712 | tf_op jit(solution)/shard_map/while/body/eval_jaxpr/cond/branch_1_fun/hgqk,khd->hgqd/dot_general | solution.py:68
  177.1 14.5 %conditional.5 = ((f32[4,2,512]{2,1,0:T(2,128)}, f32[4,2,512]{2,1,0:T(2,128)S(1)}, f32[4,2,512,256]{3,2,1,0:T(8,128)})) conditional(s32[]{:T(128)} %convert_element_type.48, (f32[4,2,512]{2,1,0:T(2,128)}, f32[4,2,512]{2,1,0:T(2,128)S(1)}, f32[4,2,512,256]{3,2,1,0:T(8,128)}) %tuple.88, (s32[]{:T(128)}, s32[]{:T(128)}, s32[512]{0:T(512)S(1)}, ...), branch_computations={%region_6.6_spmd, %region_7.9_spmd} | conditional | flops 2174495232 | bytes 39076968 | solution.py:76
  178.2 3.5 %fusion.17 = (f32[4,2,512]{2,1,0:T(2,128)S(1)}, f32[4,512,512,2]{2,1,3,0:T(8,128)S(1)}) fusion(pred[512,512]{0,1:T(8,128)(4,1)S(1)} %fusion.34, bf16[512,4,2,256]{3,0,2,1:T(8,128)(2,1)} %get-tuple-element.457, bf16[2,4096,4,256]{3,1,2,0:T(8,128)(2,1)} %get-tuple-element.456, s32[]{:T(128)S(6)} %select_n.38), kind=kOutput, calls=%fused_computation.26 | convolution fusion | flops 1080029184 | bytes 11812868 | tf_op jit(solution)/shard_map/while/body/eval_jaxpr/cond/branch_1_fun/qhgd,khd->hgqk/dot_general | solution.py:47
  181.7 0.7 max.4
  182.4 1.7 fusion.21
  184.1 0.7 multiply_add_fusion.1
  184.9 6.1 %multiply_add_fusion = f32[4,2,512,256]{3,2,1,0:T(8,128)} fusion(f32[4,2,512,256]{3,2,1,0:T(8,128)} %get-tuple-element.459, f32[4,2,512]{2,1,0:T(2,128)S(1)} %bitcast.69, f32[4,512,512,2]{2,1,3,0:T(8,128)S(1)} %get-tuple-element.549, f32[4,2,512]{2,1,0:T(2,128)S(1)} %max.4, pred[512,512]{0,1:T(8,128)(4,1)S(1)} %fusion.34, ...), kind=kOutput, calls=%fused_computation.32 | convolution fusion | flops 1084227584 | bytes 18120712 | tf_op jit(solution)/shard_map/while/body/eval_jaxpr/cond/branch_1_fun/hgqk,khd->hgqd/dot_general | solution.py:68
  192.2 14.5 %conditional.5 = ((f32[4,2,512]{2,1,0:T(2,128)}, f32[4,2,512]{2,1,0:T(2,128)S(1)}, f32[4,2,512,256]{3,2,1,0:T(8,128)})) conditional(s32[]{:T(128)} %convert_element_type.48, (f32[4,2,512]{2,1,0:T(2,128)}, f32[4,2,512]{2,1,0:T(2,128)S(1)}, f32[4,2,512,256]{3,2,1,0:T(8,128)}) %tuple.88, (s32[]{:T(128)}, s32[]{:T(128)}, s32[512]{0:T(512)S(1)}, ...), branch_computations={%region_6.6_spmd, %region_7.9_spmd} | conditional | flops 2174495232 | bytes 39076968 | solution.py:76
  193.4 3.5 %fusion.17 = (f32[4,2,512]{2,1,0:T(2,128)S(1)}, f32[4,512,512,2]{2,1,3,0:T(8,128)S(1)}) fusion(pred[512,512]{0,1:T(8,128)(4,1)S(1)} %fusion.34, bf16[512,4,2,256]{3,0,2,1:T(8,128)(2,1)} %get-tuple-element.457, bf16[2,4096,4,256]{3,1,2,0:T(8,128)(2,1)} %get-tuple-element.456, s32[]{:T(128)S(6)} %select_n.38), kind=kOutput, calls=%fused_computation.26 | convolution fusion | flops 1080029184 | bytes 11812868 | tf_op jit(solution)/shard_map/while/body/eval_jaxpr/cond/branch_1_fun/qhgd,khd->hgqk/dot_general | solution.py:47
  196.8 0.7 max.4
  197.6 1.7 fusion.21
  199.3 0.7 multiply_add_fusion.1
  200.0 6.1 %multiply_add_fusion = f32[4,2,512,256]{3,2,1,0:T(8,128)} fusion(f32[4,2,512,256]{3,2,1,0:T(8,128)} %get-tuple-element.459, f32[4,2,512]{2,1,0:T(2,128)S(1)} %bitcast.69, f32[4,512,512,2]{2,1,3,0:T(8,128)S(1)} %get-tuple-element.549, f32[4,2,512]{2,1,0:T(2,128)S(1)} %max.4, pred[512,512]{0,1:T(8,128)(4,1)S(1)} %fusion.34, ...), kind=kOutput, calls=%fused_computation.32 | convolution fusion | flops 1084227584 | bytes 18120712 | tf_op jit(solution)/shard_map/while/body/eval_jaxpr/cond/branch_1_fun/hgqk,khd->hgqd/dot_general | solution.py:68
  207.4 14.5 %conditional.5 = ((f32[4,2,512]{2,1,0:T(2,128)}, f32[4,2,512]{2,1,0:T(2,128)S(1)}, f32[4,2,512,256]{3,2,1,0:T(8,128)})) conditional(s32[]{:T(128)} %convert_element_type.48, (f32[4,2,512]{2,1,0:T(2,128)}, f32[4,2,512]{2,1,0:T(2,128)S(1)}, f32[4,2,512,256]{3,2,1,0:T(8,128)}) %tuple.88, (s32[]{:T(128)}, s32[]{:T(128)}, s32[512]{0:T(512)S(1)}, ...), branch_computations={%region_6.6_spmd, %region_7.9_spmd} | conditional | flops 2174495232 | bytes 39076968 | solution.py:76
  208.5 3.5 %fusion.17 = (f32[4,2,512]{2,1,0:T(2,128)S(1)}, f32[4,512,512,2]{2,1,3,0:T(8,128)S(1)}) fusion(pred[512,512]{0,1:T(8,128)(4,1)S(1)} %fusion.34, bf16[512,4,2,256]{3,0,2,1:T(8,128)(2,1)} %get-tuple-element.457, bf16[2,4096,4,256]{3,1,2,0:T(8,128)(2,1)} %get-tuple-element.456, s32[]{:T(128)S(6)} %select_n.38), kind=kOutput, calls=%fused_computation.26 | convolution fusion | flops 1080029184 | bytes 11812868 | tf_op jit(solution)/shard_map/while/body/eval_jaxpr/cond/branch_1_fun/qhgd,khd->hgqk/dot_general | solution.py:47
  212.0 0.7 max.4
  212.7 1.7 fusion.21
  214.5 0.7 multiply_add_fusion.1
  215.2 6.1 %multiply_add_fusion = f32[4,2,512,256]{3,2,1,0:T(8,128)} fusion(f32[4,2,512,256]{3,2,1,0:T(8,128)} %get-tuple-element.459, f32[4,2,512]{2,1,0:T(2,128)S(1)} %bitcast.69, f32[4,512,512,2]{2,1,3,0:T(8,128)S(1)} %get-tuple-element.549, f32[4,2,512]{2,1,0:T(2,128)S(1)} %max.4, pred[512,512]{0,1:T(8,128)(4,1)S(1)} %fusion.34, ...), kind=kOutput, calls=%fused_computation.32 | convolution fusion | flops 1084227584 | bytes 18120712 | tf_op jit(solution)/shard_map/while/body/eval_jaxpr/cond/branch_1_fun/hgqk,khd->hgqd/dot_general | solution.py:68
  221.9 2.6 %select_convert_fusion = bf16[4,2,512,256]{3,2,1,0:T(8,128)(2,1)S(1)} fusion(f32[4,2,512,256]{3,2,1,0:T(8,128)} %get-tuple-element.483, f32[4,2,512]{2,1,0:T(2,128)S(1)} %broadcast_select_fusion, pred[512]{0:T(512)(128)(4,1)S(1)} %broadcast_compare_fusion.5), kind=kLoop, calls=%fused_computation.57 | loop fusion | flops 3145728 | bytes 6308352 | tf_op jit(solution)/shard_map/convert_element_type | solution.py:99
  224.5 2.5 %copy.15 = bf16[512,8,256]{2,1,0:T(8,128)(2,1)} copy(bf16[512,8,256]{2,0,1:T(8,128)(2,1)S(1)} %bitcast.66) | data formatting | bytes 4194304 | tf_op jit(solution)/shard_map/convert_element_type | solution.py:99
  (48 shorter events, 13.5 us)
Async XLA Ops:
  6.5 94.1 %all-gather.2.cloned.1.call-start = ((), (), s32[]{:S(2)}) async-start(), calls=%async_computation | async-start | bytes 18874368 | tf_op jit(solution)/shard_map/all_gather | solution.py:86
Sparse Core Ops, SparseCore 0:
  10.0 90.5 all-gather.1
where the time goes:
time: 236 us; the launch traced here: 234 us
  matrix products  81.8 us (35%)
  waiting for transfers between devices  54.7 us (23%)
  other arithmetic  41.9 us (18%)
  blocking collectives  23 us (10%)
  between operations  14.1 us (6%)
  local copies, waits for them, and re-layouts  12.5 us (5%)
  loops' own time  5.89 us (2%)
    all_gather x1, waiting for transfers between devices, shards(): shard_piece = lax.all_gather(own_pair, 'seq', axis=1, tiled=True)  54.7 us
    dot_general x9, matrix products, compute(): jnp.einsum('hgqk,khd->hgqd', weights.astype(jnp.bfloat16), kv_block[1], p...  51.9 us
    dot_general x9, matrix products, compute(): jnp.einsum('qhgd,khd->hgqk', grouped, kv_block[0], preferred_element_type...  29.9 us
    psum x1, blocking collectives, spread(): return lax.psum(kept, axis)  23 us
    reduce_sum x9, other arithmetic, compute(): totals = totals * rescale + jnp.sum(weights, axis=-1)  14.7 us
    add x9, other arithmetic, compute(): totals = totals * rescale + jnp.sum(weights, axis=-1)  6.6 us
    lt x9, other arithmetic, compute(): visible = visible & (query_pos[:, None] < length_now)  5.88 us
    max x8, other arithmetic, compute(): newest = jnp.maximum(maximum, jnp.max(masked, axis=-1))  5.86 us
  transfers between devices with their start and end apart: 1, of which 1 were waited for; matrix products, arithmetic and copies ran while one was open for 5% of the time, Pallas kernels for 0%

commit v1 on v0

--- a/solution.py
+++ b/solution.py
@@ -10,7 +10,7 @@
 
 def spread(value, axis, source):
     kept = jnp.where(lax.axis_index(axis) == source, value, 0).astype(value.dtype)
-    return lax.psum(kept, axis)
+    return jnp.sum(lax.all_gather(kept, axis_name=axis), axis=0)
 
 
 def shards(queries, key_heads, projected_value_heads, lengths):

time: 236 us -> 247 us (1.047)
  waiting for transfers between devices: 54.7 us -> 70.6 us
  blocking collectives: 23 us -> 8.74 us
  local copies, waits for them, and re-layouts: 12.5 us -> 24.8 us
  matrix products: 81.8 us -> 75 us
  other arithmetic: 41.9 us -> 45.7 us
    psum x1 -> x0, blocking collectives: 23 us -> none  [spread(): return lax.psum(kept, axis)]
    all_gather x1, waiting for transfers between devices: 54.7 us -> 70.6 us  [shards(): shard_piece = lax.all_gather(own_pair, 'seq', axis=1, tiled=True)]
    unnamed x1 -> x4, local copies, waits for them, and re-layouts: 3.34 us -> 17.3 us
    all_gather x0 -> x1, blocking collectives: none -> 8.74 us  [spread(): return jnp.sum(lax.all_gather(kept, axis_name=axis), axis=0)]
    dot_general x9, matrix products: 29.9 us -> 22.7 us  [compute(): jnp.einsum('qhgd,khd->hgqk', grouped, kv_block[0], preferred_element_type...]
    another operation x1, other arithmetic: 1.5 us -> 4.43 us  [shards(): own_pair = jnp.stack([key_heads, projected_value_heads])]
  transfers between devices with their start and end apart: 1 -> 1, of which waited for: 1 -> 1; matrix products, arithmetic and copies ran while one was open for 5% -> 4% of each run, Pallas kernels for 0% -> 0%
where the time goes in v1:
time: 247 us; the launch traced here: 245 us
  matrix products  75 us (30%)
  waiting for transfers between devices  70.6 us (29%)
  other arithmetic  45.7 us (19%)
  local copies, waits for them, and re-layouts  24.8 us (10%)
  between operations  14.2 us (6%)
  blocking collectives  8.74 us (4%)
  loops' own time  5.89 us (2%)
    all_gather x1, waiting for transfers between devices, shards(): shard_piece = lax.all_gather(own_pair, 'seq', axis=1, tiled=True)  70.6 us
    dot_general x9, matrix products, compute(): jnp.einsum('hgqk,khd->hgqd', weights.astype(jnp.bfloat16), kv_block[1], p...  52.3 us
    dot_general x9, matrix products, compute(): jnp.einsum('qhgd,khd->hgqk', grouped, kv_block[0], preferred_element_type...  22.7 us
    unnamed x4, local copies, waits for them, and re-layouts  17.3 us
    reduce_sum x9, other arithmetic, compute(): totals = totals * rescale + jnp.sum(weights, axis=-1)  14.7 us
    all_gather x1, blocking collectives, spread(): return jnp.sum(lax.all_gather(kept, axis_name=axis), axis=0)  8.74 us
    add x9, other arithmetic, compute(): totals = totals * rescale + jnp.sum(weights, axis=-1)  6.6 us
    lt x9, other arithmetic, compute(): visible = visible & (query_pos[:, None] < length_now)  5.89 us
  transfers between devices with their start and end apart: 1, of which 1 were waited for; matrix products, arithmetic and copies ran while one was open for 4% of the time, Pallas kernels for 0%

profile of v1, /device:TPU:7, one launch (start us, length us, event | category | flops | bytes accessed | tf_op | source)
XLA Modules:
  0.0 244.9 jit_solution(16590603010850322827)
XLA Ops:
  6.5 4.4 %pad_maximum_fusion = bf16[2,512,4,256]{3,2,1,0:T(4,128)(2,1)} fusion(bf16[1,512,4,256]{3,2,1,0:T(4,128)(2,1)} %bitcast.68, bf16[1,512,4,256]{3,2,1,0:T(4,128)(2,1)} %bitcast.70), kind=kLoop, calls=%fused_computation.57 | loop fusion | flops 1048576 | bytes 4194304 | tf_op jit(solution)/shard_map/stack | solution.py:83
  11.7 2.0 copy.14
  13.8 0.7 fusion.36
  14.5 8.7 %all-gather = bf16[16,4,4,256]{3,2,1,0:T(4,128)(2,1)S(1)} all-gather(bf16[2,4,4,256]{3,2,1,0:T(4,128)(2,1)S(1)} %fusion.36), channel_id=2, replica_groups=mesh['batch'=4,'seq'=8] {'seq'}, dimensions={0}, use_global_device_ids=true | all-gather | bytes 147456 | tf_op jit(solution)/shard_map/all_gather | solution.py:13
  23.2 7.7 %conditional.2 = (f32[4,2,512]{2,1,0:T(2,128)}, f32[4,2,512]{2,1,0:T(2,128)S(1)}, f32[4,2,512,256]{3,2,1,0:T(8,128)}) conditional(s32[]{:T(128)} %convert_element_type.37, () %tuple.61, (s32[512]{0:T(512)S(1)}, s32[4]{0:T(128)S(1)}, s32[]{:T(128)}, s32[4]{0:T(128)S(1)}, bf16[8,2,4,4,256]{4,3,2,1,0:T(4,128)(2,1)S(1)}, ...), branch_computations={%region_0.1_spmd, %region_1.5_spmd} | conditional | flops 18055684 | bytes 6878282 | solution.py:76
  23.3 0.7 broadcast_compare_fusion.1
  23.9 0.7 broadcast_compare_fusion
  24.8 0.7 select_reduce_fusion
  26.1 0.8 fusion.4
  26.9 0.7 fusion.12
  27.6 3.3 %convolution_add_fusion = f32[4,2,512,256]{3,2,1,0:T(8,128)} fusion(f32[4,2,512]{2,1,0:T(2,128)S(1)} %get-tuple-element.557, f32[4,2,512,4]{2,3,1,0:T(4,128)S(1)} %get-tuple-element.568, f32[4,2,512]{2,1,0:T(2,128)} %get-tuple-element.656, pred[512,4]{0,1:T(4,128)(4,1)S(1)} %fusion.10, bf16[1,4,4,256]{3,2,1,0:T(4,128)(2,1)S(1)} %get-tuple-element.565), kind=kOutput, calls=%fused_computation.1 | convolution fusion | flops 9486336 | bytes 4302848 | tf_op jit(solution)/shard_map/cond/branch_1_fun/hgqk,khd->hgqd/dot_general | solution.py:68
  30.9 70.6 %all-gather.3.cloned.1.call-done = bf16[2,4096,4,256]{3,2,1,0:T(4,128)(2,1)} async-done(((bf16[2,512,4,256]{3,2,1,0:T(4,128)(2,1)}), bf16[2,4096,4,256]{3,2,1,0:T(4,128)(2,1)}) %all-gather.3.cloned.1.call-update) | async-done | bytes 16777232 | tf_op jit(solution)/shard_map/all_gather | solution.py:86
  101.5 15.3 %copy.15 = bf16[2,4096,4,256]{3,1,2,0:T(8,128)(2,1)} copy(bf16[2,4096,4,256]{3,2,1,0:T(4,128)(2,1)} %all-gather.3.cloned.1.call-done) | data formatting | bytes 33554432
  116.9 116.0 %while.22 = (s32[]{:T(128)}, f32[4,2,512]{2,1,0:T(2,128)}, f32[4,2,512]{2,1,0:T(2,128)S(1)}, f32[4,2,512,256]{3,2,1,0:T(8,128)}, s32[]{:T(128)}, /*index=5*/s32[...) while((s32[]{:T(128)}, f32[4,2,512]{2,1,0:T(2,128)}, ...), condition=%wide.region_10.11_spmd.clone, body=%wide.region_5.10_spmd.clone.sunk | while | flops 2174495232 | bytes 39079348 | solution.py:94
  117.5 13.8 %conditional.5 = ((f32[4,2,512]{2,1,0:T(2,128)}, f32[4,2,512]{2,1,0:T(2,128)S(1)}, f32[4,2,512,256]{3,2,1,0:T(8,128)})) conditional(s32[]{:T(128)} %convert_element_type.50, (f32[4,2,512]{2,1,0:T(2,128)}, f32[4,2,512]{2,1,0:T(2,128)S(1)}, f32[4,2,512,256]{3,2,1,0:T(8,128)}) %tuple.90, (s32[]{:T(128)}, s32[]{:T(128)}, s32[512]{0:T(512)S(1)}, ...), branch_computations={%region_6.6_spmd, %region_7.9_spmd} | conditional | flops 2174495232 | bytes 39076968 | solution.py:76
  118.7 2.8 %fusion.13 = (f32[4,2,512]{2,1,0:T(2,128)S(1)}, f32[4,512,512,2]{2,1,3,0:T(8,128)S(1)}) fusion(pred[512,512]{0,1:T(8,128)(4,1)S(1)} %fusion.30, bf16[512,4,2,256]{3,0,2,1:T(8,128)(2,1)S(1)} %get-tuple-element.459, bf16[2,4096,4,256]{3,1,2,0:T(8,128)(2,1)} %get-tuple-element.458, s32[]{:T(128)S(6)} %select_n.38), kind=kOutput, calls=%fused_computation.24 | convolution fusion | flops 1080029184 | bytes 11812868 | tf_op jit(solution)/shard_map/while/body/eval_jaxpr/cond/branch_1_fun/qhgd,khd->hgqk/dot_general | solution.py:47
  121.4 0.7 max.4
  122.2 1.7 fusion.17
  123.9 0.7 multiply_add_fusion.1
  124.6 6.1 %multiply_add_fusion = f32[4,2,512,256]{3,2,1,0:T(8,128)} fusion(f32[4,2,512,256]{3,2,1,0:T(8,128)} %get-tuple-element.461, f32[4,2,512]{2,1,0:T(2,128)S(1)} %bitcast.72, f32[4,512,512,2]{2,1,3,0:T(8,128)S(1)} %get-tuple-element.570, f32[4,2,512]{2,1,0:T(2,128)S(1)} %max.4, pred[512,512]{0,1:T(8,128)(4,1)S(1)} %fusion.30, ...), kind=kOutput, calls=%fused_computation.30 | convolution fusion | flops 1084227584 | bytes 18120712 | tf_op jit(solution)/shard_map/while/body/eval_jaxpr/cond/branch_1_fun/hgqk,khd->hgqd/dot_general | solution.py:68
  132.0 13.8 %conditional.5 = ((f32[4,2,512]{2,1,0:T(2,128)}, f32[4,2,512]{2,1,0:T(2,128)S(1)}, f32[4,2,512,256]{3,2,1,0:T(8,128)})) conditional(s32[]{:T(128)} %convert_element_type.50, (f32[4,2,512]{2,1,0:T(2,128)}, f32[4,2,512]{2,1,0:T(2,128)S(1)}, f32[4,2,512,256]{3,2,1,0:T(8,128)}) %tuple.90, (s32[]{:T(128)}, s32[]{:T(128)}, s32[512]{0:T(512)S(1)}, ...), branch_computations={%region_6.6_spmd, %region_7.9_spmd} | conditional | flops 2174495232 | bytes 39076968 | solution.py:76
  133.2 2.8 %fusion.13 = (f32[4,2,512]{2,1,0:T(2,128)S(1)}, f32[4,512,512,2]{2,1,3,0:T(8,128)S(1)}) fusion(pred[512,512]{0,1:T(8,128)(4,1)S(1)} %fusion.30, bf16[512,4,2,256]{3,0,2,1:T(8,128)(2,1)S(1)} %get-tuple-element.459, bf16[2,4096,4,256]{3,1,2,0:T(8,128)(2,1)} %get-tuple-element.458, s32[]{:T(128)S(6)} %select_n.38), kind=kOutput, calls=%fused_computation.24 | convolution fusion | flops 1080029184 | bytes 11812868 | tf_op jit(solution)/shard_map/while/body/eval_jaxpr/cond/branch_1_fun/qhgd,khd->hgqk/dot_general | solution.py:47
  135.9 0.7 max.4
  136.7 1.7 fusion.17
  138.4 0.7 multiply_add_fusion.1
  139.1 6.1 %multiply_add_fusion = f32[4,2,512,256]{3,2,1,0:T(8,128)} fusion(f32[4,2,512,256]{3,2,1,0:T(8,128)} %get-tuple-element.461, f32[4,2,512]{2,1,0:T(2,128)S(1)} %bitcast.72, f32[4,512,512,2]{2,1,3,0:T(8,128)S(1)} %get-tuple-element.570, f32[4,2,512]{2,1,0:T(2,128)S(1)} %max.4, pred[512,512]{0,1:T(8,128)(4,1)S(1)} %fusion.30, ...), kind=kOutput, calls=%fused_computation.30 | convolution fusion | flops 1084227584 | bytes 18120712 | tf_op jit(solution)/shard_map/while/body/eval_jaxpr/cond/branch_1_fun/hgqk,khd->hgqd/dot_general | solution.py:68
  146.5 13.8 %conditional.5 = ((f32[4,2,512]{2,1,0:T(2,128)}, f32[4,2,512]{2,1,0:T(2,128)S(1)}, f32[4,2,512,256]{3,2,1,0:T(8,128)})) conditional(s32[]{:T(128)} %convert_element_type.50, (f32[4,2,512]{2,1,0:T(2,128)}, f32[4,2,512]{2,1,0:T(2,128)S(1)}, f32[4,2,512,256]{3,2,1,0:T(8,128)}) %tuple.90, (s32[]{:T(128)}, s32[]{:T(128)}, s32[512]{0:T(512)S(1)}, ...), branch_computations={%region_6.6_spmd, %region_7.9_spmd} | conditional | flops 2174495232 | bytes 39076968 | solution.py:76
  147.7 2.8 %fusion.13 = (f32[4,2,512]{2,1,0:T(2,128)S(1)}, f32[4,512,512,2]{2,1,3,0:T(8,128)S(1)}) fusion(pred[512,512]{0,1:T(8,128)(4,1)S(1)} %fusion.30, bf16[512,4,2,256]{3,0,2,1:T(8,128)(2,1)S(1)} %get-tuple-element.459, bf16[2,4096,4,256]{3,1,2,0:T(8,128)(2,1)} %get-tuple-element.458, s32[]{:T(128)S(6)} %select_n.38), kind=kOutput, calls=%fused_computation.24 | convolution fusion | flops 1080029184 | bytes 11812868 | tf_op jit(solution)/shard_map/while/body/eval_jaxpr/cond/branch_1_fun/qhgd,khd->hgqk/dot_general | solution.py:47
  150.4 0.7 max.4
  151.2 1.7 fusion.17
  152.9 0.7 multiply_add_fusion.1
  153.6 6.1 %multiply_add_fusion = f32[4,2,512,256]{3,2,1,0:T(8,128)} fusion(f32[4,2,512,256]{3,2,1,0:T(8,128)} %get-tuple-element.461, f32[4,2,512]{2,1,0:T(2,128)S(1)} %bitcast.72, f32[4,512,512,2]{2,1,3,0:T(8,128)S(1)} %get-tuple-element.570, f32[4,2,512]{2,1,0:T(2,128)S(1)} %max.4, pred[512,512]{0,1:T(8,128)(4,1)S(1)} %fusion.30, ...), kind=kOutput, calls=%fused_computation.30 | convolution fusion | flops 1084227584 | bytes 18120712 | tf_op jit(solution)/shard_map/while/body/eval_jaxpr/cond/branch_1_fun/hgqk,khd->hgqd/dot_general | solution.py:68
  161.1 13.8 %conditional.5 = ((f32[4,2,512]{2,1,0:T(2,128)}, f32[4,2,512]{2,1,0:T(2,128)S(1)}, f32[4,2,512,256]{3,2,1,0:T(8,128)})) conditional(s32[]{:T(128)} %convert_element_type.50, (f32[4,2,512]{2,1,0:T(2,128)}, f32[4,2,512]{2,1,0:T(2,128)S(1)}, f32[4,2,512,256]{3,2,1,0:T(8,128)}) %tuple.90, (s32[]{:T(128)}, s32[]{:T(128)}, s32[512]{0:T(512)S(1)}, ...), branch_computations={%region_6.6_spmd, %region_7.9_spmd} | conditional | flops 2174495232 | bytes 39076968 | solution.py:76
  162.2 2.8 %fusion.13 = (f32[4,2,512]{2,1,0:T(2,128)S(1)}, f32[4,512,512,2]{2,1,3,0:T(8,128)S(1)}) fusion(pred[512,512]{0,1:T(8,128)(4,1)S(1)} %fusion.30, bf16[512,4,2,256]{3,0,2,1:T(8,128)(2,1)S(1)} %get-tuple-element.459, bf16[2,4096,4,256]{3,1,2,0:T(8,128)(2,1)} %get-tuple-element.458, s32[]{:T(128)S(6)} %select_n.38), kind=kOutput, calls=%fused_computation.24 | convolution fusion | flops 1080029184 | bytes 11812868 | tf_op jit(solution)/shard_map/while/body/eval_jaxpr/cond/branch_1_fun/qhgd,khd->hgqk/dot_general | solution.py:47
  164.9 0.7 max.4
  165.7 1.7 fusion.17
  167.4 0.7 multiply_add_fusion.1
  168.1 6.1 %multiply_add_fusion = f32[4,2,512,256]{3,2,1,0:T(8,128)} fusion(f32[4,2,512,256]{3,2,1,0:T(8,128)} %get-tuple-element.461, f32[4,2,512]{2,1,0:T(2,128)S(1)} %bitcast.72, f32[4,512,512,2]{2,1,3,0:T(8,128)S(1)} %get-tuple-element.570, f32[4,2,512]{2,1,0:T(2,128)S(1)} %max.4, pred[512,512]{0,1:T(8,128)(4,1)S(1)} %fusion.30, ...), kind=kOutput, calls=%fused_computation.30 | convolution fusion | flops 1084227584 | bytes 18120712 | tf_op jit(solution)/shard_map/while/body/eval_jaxpr/cond/branch_1_fun/hgqk,khd->hgqd/dot_general | solution.py:68
  175.6 13.8 %conditional.5 = ((f32[4,2,512]{2,1,0:T(2,128)}, f32[4,2,512]{2,1,0:T(2,128)S(1)}, f32[4,2,512,256]{3,2,1,0:T(8,128)})) conditional(s32[]{:T(128)} %convert_element_type.50, (f32[4,2,512]{2,1,0:T(2,128)}, f32[4,2,512]{2,1,0:T(2,128)S(1)}, f32[4,2,512,256]{3,2,1,0:T(8,128)}) %tuple.90, (s32[]{:T(128)}, s32[]{:T(128)}, s32[512]{0:T(512)S(1)}, ...), branch_computations={%region_6.6_spmd, %region_7.9_spmd} | conditional | flops 2174495232 | bytes 39076968 | solution.py:76
  176.7 2.8 %fusion.13 = (f32[4,2,512]{2,1,0:T(2,128)S(1)}, f32[4,512,512,2]{2,1,3,0:T(8,128)S(1)}) fusion(pred[512,512]{0,1:T(8,128)(4,1)S(1)} %fusion.30, bf16[512,4,2,256]{3,0,2,1:T(8,128)(2,1)S(1)} %get-tuple-element.459, bf16[2,4096,4,256]{3,1,2,0:T(8,128)(2,1)} %get-tuple-element.458, s32[]{:T(128)S(6)} %select_n.38), kind=kOutput, calls=%fused_computation.24 | convolution fusion | flops 1080029184 | bytes 11812868 | tf_op jit(solution)/shard_map/while/body/eval_jaxpr/cond/branch_1_fun/qhgd,khd->hgqk/dot_general | solution.py:47
  179.5 0.7 max.4
  180.2 1.7 fusion.17
  181.9 0.7 multiply_add_fusion.1
  182.7 6.1 %multiply_add_fusion = f32[4,2,512,256]{3,2,1,0:T(8,128)} fusion(f32[4,2,512,256]{3,2,1,0:T(8,128)} %get-tuple-element.461, f32[4,2,512]{2,1,0:T(2,128)S(1)} %bitcast.72, f32[4,512,512,2]{2,1,3,0:T(8,128)S(1)} %get-tuple-element.570, f32[4,2,512]{2,1,0:T(2,128)S(1)} %max.4, pred[512,512]{0,1:T(8,128)(4,1)S(1)} %fusion.30, ...), kind=kOutput, calls=%fused_computation.30 | convolution fusion | flops 1084227584 | bytes 18120712 | tf_op jit(solution)/shard_map/while/body/eval_jaxpr/cond/branch_1_fun/hgqk,khd->hgqd/dot_general | solution.py:68
  190.1 13.8 %conditional.5 = ((f32[4,2,512]{2,1,0:T(2,128)}, f32[4,2,512]{2,1,0:T(2,128)S(1)}, f32[4,2,512,256]{3,2,1,0:T(8,128)})) conditional(s32[]{:T(128)} %convert_element_type.50, (f32[4,2,512]{2,1,0:T(2,128)}, f32[4,2,512]{2,1,0:T(2,128)S(1)}, f32[4,2,512,256]{3,2,1,0:T(8,128)}) %tuple.90, (s32[]{:T(128)}, s32[]{:T(128)}, s32[512]{0:T(512)S(1)}, ...), branch_computations={%region_6.6_spmd, %region_7.9_spmd} | conditional | flops 2174495232 | bytes 39076968 | solution.py:76
  191.2 2.8 %fusion.13 = (f32[4,2,512]{2,1,0:T(2,128)S(1)}, f32[4,512,512,2]{2,1,3,0:T(8,128)S(1)}) fusion(pred[512,512]{0,1:T(8,128)(4,1)S(1)} %fusion.30, bf16[512,4,2,256]{3,0,2,1:T(8,128)(2,1)S(1)} %get-tuple-element.459, bf16[2,4096,4,256]{3,1,2,0:T(8,128)(2,1)} %get-tuple-element.458, s32[]{:T(128)S(6)} %select_n.38), kind=kOutput, calls=%fused_computation.24 | convolution fusion | flops 1080029184 | bytes 11812868 | tf_op jit(solution)/shard_map/while/body/eval_jaxpr/cond/branch_1_fun/qhgd,khd->hgqk/dot_general | solution.py:47
  194.0 0.7 max.4
  194.7 1.7 fusion.17
  196.4 0.7 multiply_add_fusion.1
  197.2 6.1 %multiply_add_fusion = f32[4,2,512,256]{3,2,1,0:T(8,128)} fusion(f32[4,2,512,256]{3,2,1,0:T(8,128)} %get-tuple-element.461, f32[4,2,512]{2,1,0:T(2,128)S(1)} %bitcast.72, f32[4,512,512,2]{2,1,3,0:T(8,128)S(1)} %get-tuple-element.570, f32[4,2,512]{2,1,0:T(2,128)S(1)} %max.4, pred[512,512]{0,1:T(8,128)(4,1)S(1)} %fusion.30, ...), kind=kOutput, calls=%fused_computation.30 | convolution fusion | flops 1084227584 | bytes 18120712 | tf_op jit(solution)/shard_map/while/body/eval_jaxpr/cond/branch_1_fun/hgqk,khd->hgqd/dot_general | solution.py:68
  204.6 13.8 %conditional.5 = ((f32[4,2,512]{2,1,0:T(2,128)}, f32[4,2,512]{2,1,0:T(2,128)S(1)}, f32[4,2,512,256]{3,2,1,0:T(8,128)})) conditional(s32[]{:T(128)} %convert_element_type.50, (f32[4,2,512]{2,1,0:T(2,128)}, f32[4,2,512]{2,1,0:T(2,128)S(1)}, f32[4,2,512,256]{3,2,1,0:T(8,128)}) %tuple.90, (s32[]{:T(128)}, s32[]{:T(128)}, s32[512]{0:T(512)S(1)}, ...), branch_computations={%region_6.6_spmd, %region_7.9_spmd} | conditional | flops 2174495232 | bytes 39076968 | solution.py:76
  205.7 2.8 %fusion.13 = (f32[4,2,512]{2,1,0:T(2,128)S(1)}, f32[4,512,512,2]{2,1,3,0:T(8,128)S(1)}) fusion(pred[512,512]{0,1:T(8,128)(4,1)S(1)} %fusion.30, bf16[512,4,2,256]{3,0,2,1:T(8,128)(2,1)S(1)} %get-tuple-element.459, bf16[2,4096,4,256]{3,1,2,0:T(8,128)(2,1)} %get-tuple-element.458, s32[]{:T(128)S(6)} %select_n.38), kind=kOutput, calls=%fused_computation.24 | convolution fusion | flops 1080029184 | bytes 11812868 | tf_op jit(solution)/shard_map/while/body/eval_jaxpr/cond/branch_1_fun/qhgd,khd->hgqk/dot_general | solution.py:47
  208.5 0.7 max.4
  209.2 1.7 fusion.17
  210.9 0.7 multiply_add_fusion.1
  211.7 6.1 %multiply_add_fusion = f32[4,2,512,256]{3,2,1,0:T(8,128)} fusion(f32[4,2,512,256]{3,2,1,0:T(8,128)} %get-tuple-element.461, f32[4,2,512]{2,1,0:T(2,128)S(1)} %bitcast.72, f32[4,512,512,2]{2,1,3,0:T(8,128)S(1)} %get-tuple-element.570, f32[4,2,512]{2,1,0:T(2,128)S(1)} %max.4, pred[512,512]{0,1:T(8,128)(4,1)S(1)} %fusion.30, ...), kind=kOutput, calls=%fused_computation.30 | convolution fusion | flops 1084227584 | bytes 18120712 | tf_op jit(solution)/shard_map/while/body/eval_jaxpr/cond/branch_1_fun/hgqk,khd->hgqd/dot_general | solution.py:68
  219.1 13.8 %conditional.5 = ((f32[4,2,512]{2,1,0:T(2,128)}, f32[4,2,512]{2,1,0:T(2,128)S(1)}, f32[4,2,512,256]{3,2,1,0:T(8,128)})) conditional(s32[]{:T(128)} %convert_element_type.50, (f32[4,2,512]{2,1,0:T(2,128)}, f32[4,2,512]{2,1,0:T(2,128)S(1)}, f32[4,2,512,256]{3,2,1,0:T(8,128)}) %tuple.90, (s32[]{:T(128)}, s32[]{:T(128)}, s32[512]{0:T(512)S(1)}, ...), branch_computations={%region_6.6_spmd, %region_7.9_spmd} | conditional | flops 2174495232 | bytes 39076968 | solution.py:76
  220.2 2.8 %fusion.13 = (f32[4,2,512]{2,1,0:T(2,128)S(1)}, f32[4,512,512,2]{2,1,3,0:T(8,128)S(1)}) fusion(pred[512,512]{0,1:T(8,128)(4,1)S(1)} %fusion.30, bf16[512,4,2,256]{3,0,2,1:T(8,128)(2,1)S(1)} %get-tuple-element.459, bf16[2,4096,4,256]{3,1,2,0:T(8,128)(2,1)} %get-tuple-element.458, s32[]{:T(128)S(6)} %select_n.38), kind=kOutput, calls=%fused_computation.24 | convolution fusion | flops 1080029184 | bytes 11812868 | tf_op jit(solution)/shard_map/while/body/eval_jaxpr/cond/branch_1_fun/qhgd,khd->hgqk/dot_general | solution.py:47
  223.0 0.7 max.4
  223.7 1.7 fusion.17
  225.4 0.7 multiply_add_fusion.1
  226.2 6.1 %multiply_add_fusion = f32[4,2,512,256]{3,2,1,0:T(8,128)} fusion(f32[4,2,512,256]{3,2,1,0:T(8,128)} %get-tuple-element.461, f32[4,2,512]{2,1,0:T(2,128)S(1)} %bitcast.72, f32[4,512,512,2]{2,1,3,0:T(8,128)S(1)} %get-tuple-element.570, f32[4,2,512]{2,1,0:T(2,128)S(1)} %max.4, pred[512,512]{0,1:T(8,128)(4,1)S(1)} %fusion.30, ...), kind=kOutput, calls=%fused_computation.30 | convolution fusion | flops 1084227584 | bytes 18120712 | tf_op jit(solution)/shard_map/while/body/eval_jaxpr/cond/branch_1_fun/hgqk,khd->hgqd/dot_general | solution.py:68
  232.9 2.6 %select_convert_fusion = bf16[4,2,512,256]{3,2,1,0:T(8,128)(2,1)S(1)} fusion(f32[4,2,512,256]{3,2,1,0:T(8,128)} %get-tuple-element.485, f32[4,2,512]{2,1,0:T(2,128)S(1)} %broadcast_select_fusion, pred[512]{0:T(512)(128)(4,1)S(1)} %broadcast_compare_fusion.5), kind=kLoop, calls=%fused_computation.55 | loop fusion | flops 3145728 | bytes 6308352 | tf_op jit(solution)/shard_map/convert_element_type | solution.py:99
  235.6 2.5 %copy.22 = bf16[512,8,256]{2,1,0:T(8,128)(2,1)} copy(bf16[512,8,256]{2,0,1:T(8,128)(2,1)S(1)} %bitcast.65) | data formatting | bytes 4194304 | tf_op jit(solution)/shard_map/convert_element_type | solution.py:99
  (52 shorter events, 14.5 us)
Async XLA Ops:
  6.5 95.0 %all-gather.3.cloned.1.call-start = ((), (), s32[]{:S(2)}) async-start(), calls=%async_computation | async-start | bytes 18874368 | tf_op jit(solution)/shard_map/all_gather | solution.py:86
  11.0 2.8 %copy-start = (bf16[512,4,256]{2,1,0:T(4,128)(2,1)S(1)}, bf16[512,4,256]{2,1,0:T(4,128)(2,1)}, u32[]{:S(2)}) copy-start(bf16[512,4,256]{2,1,0:T(4,128)(2,1)} %param.12) | copy-start | bytes 3145732
Sparse Core Ops, SparseCore 0:
  11.1 90.3 all-gather.2
